TPU v7x, 256 devices: a whole 4x4x8 slice. The times are simulated.
256 devices in a mesh: band: 4 (over x), tile: 64 (over y, z, core).
Axes of the slice: x: 4, y: 4, z: 8, core: 2. Of those that a mesh axis runs over, the one named last changes fastest.
Arguments:
- granules: bfloat16 [1024, 16, 4096], P('tile', 'band'), may hold values from -6 to 6
- valid_rows: int32 [1024, 64], P('tile'), may hold values 0 or 1
- scene_order: int32 [1024], P('tile'), may hold values from 0 to 1023, each once
- intersections: int32 [1024, 4], P('tile'), may hold values from 0 to 63, all different within a row; in each aligned block of 16 rows (0 to 15, 16 to 31, ...) at most 2 rows name the same one
- row_resample: bfloat16 [1024, 4, 4096], P('tile'), may hold values from 0 to 1.4, as said below
- col_resample: bfloat16 [1024, 4, 4096], P('tile'), may hold values from 0 to 1.4, as said below
- w_in: bfloat16 [16, 256], replicated, may hold values from -1.5 to 1.5
- w_hidden: bfloat16 [2, 256, 256], replicated, may hold values from -0.375 to 0.375
- w_out: bfloat16 [256], replicated, may hold values from -1.5 to 1.5
Outputs:
- composite: float32 [16, 262144], P('band', 'tile')
Inputs may be any that keep to these rules, and one draw needn't show every extreme that they name: `intersections`: each scene names 4 different output tiles; the 16 scenes of one device name any one tile at most 2 times, a bound that some block reaches. `scene_order`: each order number appears once. `row_resample`: nonnegative resampling weights. `col_resample`: nonnegative resampling weights.
All inputs are finite; a program needn't handle non-finite values. No bound on the sum of `valid_rows` on one device may be relied on, other than what follows from the above.
Results may differ from a plain program's by a relative error of at most 0.0031.
Values may be sent and summed in bfloat16 or wider, within the bound.
No kernel may reach another device: no remote copies, remote signals or barrier semaphores. Data moves between devices by JAX's collectives and lax.ppermute only.
A program may use at most 128 MiB of HBM per device.

v0:
```python
import jax
import jax.numpy as jnp
from jax import lax
from jax.sharding import PartitionSpec as P

HUBER_ITERS = 4
SMOOTH = 2
prior_weight = 0.25
huber_delta = 0.5
edge_scale = 1.0
smooth_rate = 0.2


def extended_2(block, sides, width):
    for axis, dim in sides:
        count = lax.axis_size(axis)
        forward = [(i, i + 1) for i in range(count - 1)]
        backward = [(target, source) for source, target in forward]
        low = lax.ppermute(
            lax.slice_in_dim(block, block.shape[dim] - width, None, axis=dim), axis, forward
        )
        high = lax.ppermute(lax.slice_in_dim(block, 0, width, axis=dim), axis, backward)
        block = jnp.concatenate([low, block, high], axis=dim)
    return block


def scene_weights(pixels, valid_part, recency, w_in, w_hidden, w_out, side_cells):
    scenes, row_count = valid_part.shape
    valid_pix = jnp.broadcast_to(
        valid_part.astype(jnp.float32)[:, :, None], (scenes, row_count, side_cells)
    )
    valid_pix = valid_pix.reshape(scenes, row_count * side_cells)

    def one_scene(inputs):
        scene_pixels, scene_valid, scene_recency = inputs
        hidden = jax.nn.silu(
            jnp.einsum("cn,ch->nh", scene_pixels, w_in, preferred_element_type=jnp.float32)
        ).astype(jnp.bfloat16)
        for repeat in range(w_hidden.shape[0]):
            hidden = jax.nn.silu(
                jnp.dot(hidden, w_hidden[repeat], preferred_element_type=jnp.float32)
            ).astype(jnp.bfloat16)
        logits = jnp.dot(hidden, w_out, preferred_element_type=jnp.float32)
        return (jax.nn.sigmoid(-logits) * scene_valid * scene_recency).astype(jnp.bfloat16)

    return lax.map(one_scene, (pixels, valid_pix, recency))


def reproject(planes, rows_matrix, cols_matrix):
    half_done = jnp.einsum(
        "ncil,njl->ncij", planes, cols_matrix, preferred_element_type=jnp.float32
    ).astype(jnp.bfloat16)
    return jnp.einsum(
        "nij,ncjl->ncil", rows_matrix, half_done, preferred_element_type=jnp.float32
    ).astype(jnp.bfloat16)


def huber_merge(observed, weights):
    values = observed.astype(jnp.float32)
    plain = weights.astype(jnp.float32)[:, None, :]
    estimate = jnp.sum(plain * values, 0) / (jnp.sum(plain, 0) + prior_weight)
    for repeat in range(HUBER_ITERS):
        residual = values - estimate[None]
        huber_w = plain * huber_delta / jnp.maximum(jnp.abs(residual), huber_delta)
        estimate = jnp.sum(huber_w * values, 0) / (jnp.sum(huber_w, 0) + prior_weight)
    return estimate


def smooth_step(extended, first_col, total_cols):
    positions = first_col + jnp.arange(extended.shape[2] - 1)
    inside = ((positions >= 0) & (positions + 1 < total_cols)).astype(jnp.float32)
    across = extended[:, :, 1:] - extended[:, :, :-1]
    sideways = across / (1.0 + (across / edge_scale) ** 2) * inside
    centre = extended[:, :, 1:-1]
    upward_diff = centre[:, 1:, :] - centre[:, :-1, :]
    upward = upward_diff / (1.0 + (upward_diff / edge_scale) ** 2)
    zeros_row = jnp.zeros_like(upward[:, :1, :])
    vertical = jnp.concatenate([upward, zeros_row], 1) - jnp.concatenate([zeros_row, upward], 1)
    return centre + smooth_rate * (sideways[:, :, 1:] - sideways[:, :, :-1] + vertical)


def per_device(
    granules,
    valid_rows,
    scene_order,
    intersections,
    row_resample,
    col_resample,
    w_in,
    w_hidden,
    w_out,
):
    scenes, group_bands, pixel_count = granules.shape
    side_cells = valid_rows.shape[1]
    intersection_count = intersections.shape[1]
    tile_count = lax.axis_size("tile")
    band_count = lax.axis_size("band")
    recency = jnp.exp(1.4 * scene_order.astype(jnp.float32) / (scenes * tile_count) - 0.7)
    by_rows = lax.all_to_all(granules, "band", split_axis=2, concat_axis=1, tiled=True)
    row_count = side_cells // band_count
    valid_here = lax.dynamic_slice_in_dim(
        valid_rows, lax.axis_index("band") * row_count, row_count, 1
    )
    partial_weights = scene_weights(by_rows, valid_here, recency, w_in, w_hidden, w_out, side_cells)
    weights = lax.all_gather(partial_weights, "band", axis=1, tiled=True)
    plane_count = group_bands + 1
    planes = jnp.concatenate([granules, weights[:, None, :]], 1)
    entry_count = scenes * intersection_count
    capacity = (entry_count + tile_count - 1) // tile_count + 1
    buffer_rows = tile_count * capacity
    flat_dest = intersections.reshape(entry_count)
    onehot = (flat_dest[:, None] == jnp.arange(tile_count, dtype=jnp.int32)[None, :]).astype(
        jnp.int32
    )
    slot_rank = jnp.sum((jnp.cumsum(onehot, 0) - onehot) * onehot, 1)
    slot_index = flat_dest * capacity + slot_rank
    raw_planes = jnp.repeat(planes, intersection_count, axis=0)
    matrices = jnp.stack([row_resample, col_resample], 2).reshape(entry_count, 2, pixel_count)
    raw_out = (
        jnp.zeros((buffer_rows, plane_count, pixel_count), jnp.bfloat16)
        .at[slot_index]
        .set(raw_planes)
    )
    matrix_out = jnp.zeros((buffer_rows, 2, pixel_count), jnp.bfloat16).at[slot_index].set(matrices)
    raw_in, matrix_in = (
        lax.all_to_all(raw_out, "tile", split_axis=0, concat_axis=0, tiled=True),
        lax.all_to_all(matrix_out, "tile", split_axis=0, concat_axis=0, tiled=True),
    )
    matrix_in = matrix_in.reshape(buffer_rows, 2, side_cells, side_cells)
    incoming = reproject(
        raw_in.reshape(buffer_rows, plane_count, side_cells, side_cells),
        matrix_in[:, 0],
        matrix_in[:, 1],
    )
    incoming = incoming.reshape(buffer_rows, plane_count, pixel_count)
    estimate = huber_merge(incoming[:, :group_bands], incoming[:, group_bands])
    field = estimate.reshape(group_bands, side_cells, side_cells)
    first_col = lax.axis_index("tile") * side_cells
    total_cols = tile_count * side_cells
    for repeat in range(SMOOTH):
        extended = extended_2(field, (("tile", 2),), 1)
        field = smooth_step(extended, first_col - 1, total_cols)
    return field.reshape(group_bands, pixel_count)


def solution(mesh):
    return jax.shard_map(
        per_device,
        mesh=mesh,
        in_specs=(
            P("tile", "band", None),
            P("tile", None),
            P("tile"),
            P("tile", None),
            P("tile", None, None),
            P("tile", None, None),
            P(),
            P(),
            P(),
        ),
        out_specs=P("band", "tile"),
        check_vma=False,
    )
```

profile of v0, /device:TPU:8, one launch (start us, length us, event | category | flops | bytes accessed | tf_op | source)
XLA Modules:
  0.0 474.6 jit_solution(6735166915798410247)
XLA Ops:
  0.0 6.5 %copy.57 = bf16[16,4,4096]{0,1,2:T(4,128)(2,1)} copy(bf16[16,4,4096]{2,1,0:T(4,128)(2,1)} %param.11) | data formatting | bytes 1048576 | tf_op args[0]
  6.5 6.5 %reshape.136 = bf16[4,2,32768]{2,1,0:T(2,128)(2,1)} reshape(bf16[4096,4,16]{2,1,0:T(4,128)(2,1)} %bitcast.84) | data formatting | bytes 1048576
  13.0 4.3 all-to-all-start
  19.9 2.4 pad_maximum_fusion.1
  22.3 3.4 broadcast_in_dim.40
  25.8 8.2 %scatter_fusion.1 = bf16[128,2,4096]{2,1,0:T(2,128)(2,1)} fusion(bf16[128,2,4096]{2,1,0:T(2,128)(2,1)} %broadcast_in_dim.40, s32[64]{0:T(128)S(1)} %fusion.59, bf16[64,2,4096]{2,1,0:T(2,128)(2,1)S(1)} %pad_maximum_fusion.1), kind=kCustom, calls=%fused_computation.1 | custom fusion | bytes 3145984 | tf_op jit(solution)/shard_map/scatter | solution.py:124
  34.0 12.1 %all-to-all-start.2 = ((bf16[128,2,4096]{2,1,0:T(2,128)(2,1)}), bf16[128,2,4096]{2,1,0:T(2,128)(2,1)S(1)}, u32[]{:S(2)}, u32[]{:S(2)}) async-start(bf16[128,2,4096]{2,1,0:T(2,128)(2,1)} %scatter_fusion.1), calls=%async_computation.2 | async-start | bytes 4194304 | tf_op jit(solution)/shard_map/all_to_all | solution.py:127
  46.1 5.4 %reshape.137 = bf16[4096,4,16]{2,1,0:T(4,128)(2,1)} reshape(bf16[4,2,32768]{2,1,0:T(2,128)(2,1)} %all-to-all-done) | data formatting | bytes 1048576
  51.5 6.1 %copy.58 = bf16[16,4,4,1024]{3,2,1,0:T(4,128)(2,1)S(1)} copy(bf16[16,4,4,1024]{0,2,3,1:T(4,128)(2,1)} %bitcast.83) | data formatting | bytes 1048576 | tf_op jit(solution)/shard_map/all_to_all | solution.py:99
  57.8 74.0 %while.10 = (s32[]{:T(128)}, bf16[16,1024]{1,0:T(8,128)(2,1)S(1)}, bf16[16,16,1024]{2,1,0:T(8,128)(2,1)S(1)}, bf16[16,256]{1,0:T(8,128)(2,1)S(1)}, bf16[2,256,25...) while((s32[]{:T(128)}, bf16[16,1024]{1,0:T(8,128)(2,1)S(1)}, ...), condition=%wide.region_3.4_spmd, body=%wide.region_2.3_spmd.sunk | while | flops 281285632 | bytes 1384577 | solution.py:46
  59.3 1.6 fusion.80
  63.9 1.6 fusion.80
  68.6 1.6 fusion.80
  77.8 1.6 fusion.80
  82.4 1.6 fusion.80
  87.0 1.6 fusion.80
  91.7 1.6 fusion.80
  96.3 1.6 fusion.80
  100.9 1.6 fusion.80
  119.4 1.6 fusion.80
  124.0 1.6 fusion.80
  128.7 1.6 fusion.80
  131.7 12.8 %all_gather.3 = bf16[16,4096]{1,0:T(8,128)(2,1)S(1)} all-gather(bf16[16,1024]{1,0:T(8,128)(2,1)S(1)} %get-tuple-element.47), channel_id=1, replica_groups=mesh['band'=4,'tile'=64] {'band'}, dimensions={1}, use_global_device_ids=true | all-gather | bytes 163840 | tf_op jit(solution)/shard_map/all_gather | solution.py:105
  145.4 2.4 broadcast_in_dim.20.clone
  147.8 4.3 broadcast_in_dim.16
  152.1 11.9 %scatter_fusion = bf16[128,5,4096]{2,1,0:T(8,128)(2,1)} fusion(bf16[128,5,4096]{2,1,0:T(8,128)(2,1)} %broadcast_in_dim.16, s32[64]{0:T(128)S(1)} %fusion.59, bf16[64,5,4096]{2,1,0:T(8,128)(2,1)} %bitcast.82), kind=kCustom, calls=%fused_computation | custom fusion | bytes 7864576 | tf_op jit(solution)/shard_map/scatter | solution.py:122
  164.0 10.5 %all-to-all-start.1 = ((bf16[128,5,4096]{2,1,0:T(8,128)(2,1)}), bf16[128,5,4096]{2,1,0:T(8,128)(2,1)}, u32[]{:S(2)}, u32[]{:S(2)}) async-start(bf16[128,5,4096]{2,1,0:T(8,128)(2,1)} %scatter_fusion), calls=%async_computation.1 | async-start | bytes 16777216 | tf_op jit(solution)/shard_map/all_to_all | solution.py:126
  174.5 4.0 copy.65
  178.6 2.7 fusion.60
  181.3 3.9 copy.75
  185.2 3.8 copy.76
  189.0 169.8 %all-to-all-done.1 = bf16[128,5,4096]{2,1,0:T(8,128)(2,1)} async-done(((bf16[128,5,4096]{2,1,0:T(8,128)(2,1)}), bf16[128,5,4096]{2,1,0:T(8,128)(2,1)}, u32[]{:S(2)}, u32[]{:S(2)}) %all-to-all-start.1) | async-done | bytes 5242912 | tf_op jit(solution)/shard_map/all_to_all | solution.py:126
  358.8 10.6 %copy.62 = bf16[128,5,4096]{0,2,1:T(8,128)(2,1)} copy(bf16[128,5,4096]{2,1,0:T(8,128)(2,1)} %all-to-all-done.1) | data formatting | bytes 10485760 | tf_op jit(solution)/shard_map/all_to_all | solution.py:126
  369.5 15.7 %copy.67 = bf16[128,5,64,64]{3,2,1,0:T(8,128)(2,1)} copy(bf16[128,5,64,64]{0,3,2,1:T(8,128)(2,1)} %bitcast.81) | data formatting | bytes 10485760 | tf_op jit(solution)/shard_map/reshape | solution.py:131
  385.2 12.5 %convert_bitcast_fusion = bf16[128,5,64,64]{2,3,1,0:T(8,128)(2,1)} fusion(bf16[128,5,64,64]{3,2,1,0:T(8,128)(2,1)} %copy.67, bf16[128,1,64,64]{3,2,0,1:T(8,128)(2,1)} %copy.76, bf16[128,1,64,64]{3,2,0,1:T(8,128)(2,1)S(1)} %copy.75), kind=kOutput, calls=%fused_computation.29 | convolution fusion | flops 676331520 | bytes 12582912 | tf_op jit(solution)/shard_map/nij,ncjl->ncil/dot_general | solution.py:53
  397.7 18.1 %copy.70 = bf16[128,5,64,64]{0,3,2,1:T(8,128)(2,1)} copy(bf16[128,5,64,64]{2,3,1,0:T(8,128)(2,1)} %convert_bitcast_fusion) | data formatting | bytes 10485760 | tf_op jit(solution)/shard_map/convert_element_type | solution.py:55
  417.3 1.9 fusion.48
  419.3 2.3 fusion.23
  421.6 7.8 %fusion.47 = (f32[4,4096]{1,0:T(4,128)S(1)}, f32[4,4096]{1,0:T(4,128)S(1)}) fusion(f32[4,4096]{1,0:T(4,128)S(1)} %broadcast_divide_fusion, f32[128,4096]{0,1:T(8,128)S(1)} %get-tuple-element.72, bf16[128,5,4096]{0,2,1:T(8,128)(2,1)S(1)} %bitcast.77), kind=kLoop, calls=%fused_computation.53 | loop fusion | flops 16744448 | bytes 6488064 | tf_op jit(solution)/shard_map/reduce_sum | solution.py:65
  429.4 7.6 %fusion.46 = (f32[4,4096]{1,0:T(4,128)S(1)}, f32[4,4096]{1,0:T(4,128)S(1)}) fusion(f32[4,4096]{1,0:T(4,128)S(1)} %add_divide_fusion.5, f32[128,4096]{0,1:T(8,128)S(1)} %get-tuple-element.72, bf16[128,5,4096]{0,2,1:T(8,128)(2,1)S(1)} %bitcast.78), kind=kLoop, calls=%fused_computation.52 | loop fusion | flops 16744448 | bytes 6488064 | tf_op jit(solution)/shard_map/reduce_sum | solution.py:65
  437.1 7.6 %fusion.45 = (f32[4,4096]{1,0:T(4,128)S(1)}, f32[4,4096]{1,0:T(4,128)S(1)}) fusion(f32[4,4096]{1,0:T(4,128)S(1)} %add_divide_fusion.4, f32[128,4096]{0,1:T(8,128)S(1)} %get-tuple-element.72, bf16[128,5,4096]{0,2,1:T(8,128)(2,1)S(1)} %bitcast.79), kind=kLoop, calls=%fused_computation.51 | loop fusion | flops 16744448 | bytes 6488064 | tf_op jit(solution)/shard_map/reduce_sum | solution.py:65
  444.7 7.6 %fusion.44 = (f32[4,4096]{1,0:T(4,128)S(1)}, f32[4,4096]{1,0:T(4,128)S(1)}) fusion(f32[4,4096]{1,0:T(4,128)S(1)} %add_divide_fusion.3, f32[128,4096]{0,1:T(8,128)S(1)} %get-tuple-element.72, bf16[128,5,4096]{0,2,1:T(8,128)(2,1)S(1)} %bitcast.80), kind=kLoop, calls=%fused_computation.50 | loop fusion | flops 16744448 | bytes 6488064 | tf_op jit(solution)/shard_map/reduce_sum | solution.py:65
  452.6 1.9 collective-permute-start
  454.5 3.3 collective-permute-start.1
  457.8 5.1 %collective-permute-done.1 = f32[4,64,1]{2,1,0:T(8,128)S(1)} collective-permute-done((f32[4,64,1]{2,1,0:T(8,128)S(1)}, f32[4,64,1]{2,1,0:T(8,128)S(1)}, u32[]{:S(2)}, u32[]{:S(2)}) %collective-permute-start.1) | collective-permute-done | bytes 1056 | tf_op jit(solution)/shard_map/ppermute | solution.py:19
  463.3 1.9 collective-permute-start.2
  465.2 2.4 collective-permute-start.3
  467.7 5.9 %collective-permute-done.3 = f32[4,64,1]{2,1,0:T(8,128)S(1)} collective-permute-done((f32[4,64,1]{2,1,0:T(8,128)S(1)}, f32[4,64,1]{2,1,0:T(8,128)S(1)}, u32[]{:S(2)}, u32[]{:S(2)}) %collective-permute-start.3) | collective-permute-done | bytes 1056 | tf_op jit(solution)/shard_map/ppermute | solution.py:19
  (177 shorter events, 61.0 us)
Async XLA Ops:
  0.0 17.3 %copy-start.4 = (s32[16,4]{0,1:T(4,128)S(1)}, s32[16,4]{0,1:T(4,128)}, u32[]{:S(2)}) copy-start(s32[16,4]{0,1:T(4,128)} %param.14) | copy-start | bytes 772
  0.0 17.4 %copy-start.5 = (s32[16,64]{1,0:T(8,128)S(1)}, s32[16,64]{1,0:T(8,128)}, u32[]{:S(2)}) copy-start(s32[16,64]{1,0:T(8,128)} %param.12) | copy-start | bytes 12292
  0.0 18.3 %copy-start.2 = (bf16[16,4,4096]{2,1,0:T(4,128)(2,1)S(1)}, bf16[16,4,4096]{2,1,0:T(4,128)(2,1)}, u32[]{:S(2)}) copy-start(bf16[16,4,4096]{2,1,0:T(4,128)(2,1)} %param.15) | copy-start | bytes 1572868
  0.0 19.1 %copy-start.3 = (bf16[16,4,4096]{2,1,0:T(4,128)(2,1)S(1)}, bf16[16,4,4096]{2,1,0:T(4,128)(2,1)}, u32[]{:S(2)}) copy-start(bf16[16,4,4096]{2,1,0:T(4,128)(2,1)} %param.16) | copy-start | bytes 1572868
  6.5 27.5 %copy-start.8 = (s32[16]{0:T(128)S(1)}, s32[16]{0:T(128)}, u32[]{:S(2)}) copy-start(s32[16]{0:T(128)} %param.13) | copy-start | bytes 196
  13.0 21.0 %all-to-all-start = ((bf16[4,2,32768]{2,1,0:T(2,128)(2,1)}), bf16[4,2,32768]{2,1,0:T(2,128)(2,1)}, u32[]{:S(2)}, u32[]{:S(2)}) async-start(bf16[4,2,32768]{2,1,0:T(2,128)(2,1)} %reshape.136), calls=%async_computation | async-start | bytes 1048576 | tf_op jit(solution)/shard_map/all_to_all | solution.py:99
  25.8 32.0 %copy-start.6 = (bf16[2,256,256]{2,1,0:T(8,128)(2,1)S(1)}, bf16[2,256,256]{2,1,0:T(8,128)(2,1)}, u32[]{:S(2)}) copy-start(bf16[2,256,256]{2,1,0:T(8,128)(2,1)} %param.18) | copy-start | bytes 786436
  25.8 32.0 %copy-start.7 = (bf16[16,256]{1,0:T(8,128)(2,1)S(1)}, bf16[16,256]{1,0:T(8,128)(2,1)}, u32[]{:S(2)}) copy-start(bf16[16,256]{1,0:T(8,128)(2,1)} %param.17) | copy-start | bytes 24580
  25.8 32.0 %copy-start.9 = (bf16[256]{0:T(256)(128)(2,1)S(1)}, bf16[256]{0:T(256)(128)(2,1)}, u32[]{:S(2)}) copy-start(bf16[256]{0:T(256)(128)(2,1)} %param.19) | copy-start | bytes 1540
  34.0 130.0 %all-to-all-start.2 = ((bf16[128,2,4096]{2,1,0:T(2,128)(2,1)}), bf16[128,2,4096]{2,1,0:T(2,128)(2,1)S(1)}, u32[]{:S(2)}, u32[]{:S(2)}) async-start(bf16[128,2,4096]{2,1,0:T(2,128)(2,1)} %scatter_fusion.1), calls=%async_computation.2 | async-start | bytes 4194304 | tf_op jit(solution)/shard_map/all_to_all | solution.py:127
  57.7 87.1 %copy-start.1 = (bf16[16,4,4096]{2,1,0:T(4,128)(2,1)S(1)}, bf16[16,4,4096]{2,1,0:T(4,128)(2,1)}, u32[]{:S(2)}) copy-start(bf16[16,4,4096]{2,1,0:T(4,128)(2,1)} %param.11) | copy-start | bytes 1572868
  164.0 194.8 %all-to-all-start.1 = ((bf16[128,5,4096]{2,1,0:T(8,128)(2,1)}), bf16[128,5,4096]{2,1,0:T(8,128)(2,1)}, u32[]{:S(2)}, u32[]{:S(2)}) async-start(bf16[128,5,4096]{2,1,0:T(8,128)(2,1)} %scatter_fusion), calls=%async_computation.1 | async-start | bytes 16777216 | tf_op jit(solution)/shard_map/all_to_all | solution.py:126
  415.8 3.4 copy-start
  452.6 5.3 %collective-permute-start = (f32[4,64,1]{2,1,0:T(8,128)S(1)}, f32[4,64,1]{2,1,0:T(8,128)S(1)}, u32[]{:S(2)}, u32[]{:S(2)}) collective-permute-start(f32[4,64,1]{2,1,0:T(8,128)S(1)} %get-tuple-element.78), channel_id=1, source_target_pairs={{1,0},{2,1},{3,2},{4,3},{5,4},{6,5},{7,6},{8,7},{9,8},{10,9},{11,1... | collective-permute-start | bytes 3080 | tf_op jit(solution)/shard_map/ppermute | solution.py:22
  454.5 8.4 %collective-permute-start.1 = (f32[4,64,1]{2,1,0:T(8,128)S(1)}, f32[4,64,1]{2,1,0:T(8,128)S(1)}, u32[]{:S(2)}, u32[]{:S(2)}) collective-permute-start(f32[4,64,1]{2,1,0:T(8,128)S(1)} %get-tuple-element.79), channel_id=1, source_target_pairs={{0,1},{1,2},{2,3},{3,4},{4,5},{5,6},{6,7},{7,8},{8,9},{9,10},{10,1... | collective-permute-start | bytes 3080 | tf_op jit(solution)/shard_map/ppermute | solution.py:19
  463.3 4.4 collective-permute-start.2
  465.2 8.4 %collective-permute-start.3 = (f32[4,64,1]{2,1,0:T(8,128)S(1)}, f32[4,64,1]{2,1,0:T(8,128)S(1)}, u32[]{:S(2)}, u32[]{:S(2)}) collective-permute-start(f32[4,64,1]{2,1,0:T(8,128)S(1)} %get-tuple-element.77), channel_id=1, source_target_pairs={{0,1},{1,2},{2,3},{3,4},{4,5},{5,6},{6,7},{7,8},{8,9},{9,10},{10,1... | collective-permute-start | bytes 3080 | tf_op jit(solution)/shard_map/ppermute | solution.py:19
where the time goes:
time: 477 us; the launch traced here: 475 us
  waiting for transfers between devices  181 us (38%)
  local copies, waits for them, and re-layouts  129 us (27%)
  matrix products  62.6 us (13%)
  other arithmetic  51.6 us (11%)
  starting transfers between devices  36.4 us (8%)
  blocking collectives  12.8 us (3%)
    all_to_all x1, waiting for transfers between devices, per_device(): lax.all_to_all(raw_out, 'tile', split_axis=0, concat_axis=0, tiled=True)  170 us
    reduce_sum x4, other arithmetic, huber_merge(): jnp.sum(huber_w, 0) + prior_weight  30.6 us
    unnamed x26, local copies, waits for them, and re-layouts  26.2 us
    dot_general x16, matrix products, one_scene(): logits = jnp.dot(hidden, w_out, preferred_element_type=jnp.float32)  25.4 us
    dot_general x16, matrix products, one_scene(): jnp.dot(hidden, w_hidden[repeat], preferred_element_type=jnp.float32)  24.6 us
    convert_element_type x1, local copies, waits for them, and re-layouts, reproject(): return jnp.einsum('nij,ncjl->ncil', rows_matrix, half_done, preferred_ele...  18.1 us
    reshape x1, local copies, waits for them, and re-layouts, per_device(): raw_in.reshape(buffer_rows, plane_count, side_cells, side_cells)  15.7 us
    all_gather x1, blocking collectives, per_device(): weights = lax.all_gather(partial_weights, 'band', axis=1, tiled=True)  12.8 us
  transfers between devices with their start and end apart: 7, of which 3 were waited for; matrix products, arithmetic and copies ran while one was open for 29% of the time, Pallas kernels for 0%

commit v1 on v0

--- a/solution.py
+++ b/solution.py
@@ -96,7 +96,9 @@
     tile_count = lax.axis_size("tile")
     band_count = lax.axis_size("band")
     recency = jnp.exp(1.4 * scene_order.astype(jnp.float32) / (scenes * tile_count) - 0.7)
-    by_rows = lax.all_to_all(granules, "band", split_axis=2, concat_axis=1, tiled=True)
+    pieces = jnp.split(granules, lax.axis_size("band"), axis=2)
+    got = lax.all_to_all(jnp.stack(pieces), "band", 0, 0)
+    by_rows = jnp.concatenate(got, axis=1)
     row_count = side_cells // band_count
     valid_here = lax.dynamic_slice_in_dim(
         valid_rows, lax.axis_index("band") * row_count, row_count, 1

time: 477 us -> 462 us (0.969)
  local copies, waits for them, and re-layouts: 129 us -> 111 us
    unnamed x26 -> x15, local copies, waits for them, and re-layouts: 26.2 us -> 8.52 us
    all_to_all x2 -> x0, local copies, waits for them, and re-layouts: 6.2 us -> none  [per_device(): lax.all_to_all(granules, 'band', split_axis=2, concat_axis=1, tiled=True)]
  transfers between devices with their start and end apart: 7 -> 7, of which waited for: 3 -> 3; matrix products, arithmetic and copies ran while one was open for 29% -> 28% of each run, Pallas kernels for 0% -> 0%
where the time goes in v1:
time: 462 us; the launch traced here: 459 us
  waiting for transfers between devices  181 us (39%)
  local copies, waits for them, and re-layouts  111 us (24%)
  matrix products  62.5 us (14%)
  other arithmetic  54.2 us (12%)
  starting transfers between devices  36.4 us (8%)
  blocking collectives  12.8 us (3%)
    all_to_all x1, waiting for transfers between devices, per_device(): lax.all_to_all(raw_out, 'tile', split_axis=0, concat_axis=0, tiled=True)  170 us
    reduce_sum x4, other arithmetic, huber_merge(): jnp.sum(huber_w, 0) + prior_weight  30.6 us
    dot_general x16, matrix products, one_scene(): logits = jnp.dot(hidden, w_out, preferred_element_type=jnp.float32)  25.4 us
    dot_general x16, matrix products, one_scene(): jnp.dot(hidden, w_hidden[repeat], preferred_element_type=jnp.float32)  24.6 us
    convert_element_type x1, local copies, waits for them, and re-layouts, reproject(): return jnp.einsum('nij,ncjl->ncil', rows_matrix, half_done, preferred_ele...  18.1 us
    reshape x1, local copies, waits for them, and re-layouts, per_device(): raw_in.reshape(buffer_rows, plane_count, side_cells, side_cells)  15.7 us
    all_gather x1, blocking collectives, per_device(): weights = lax.all_gather(partial_weights, 'band', axis=1, tiled=True)  12.8 us
    dot_general x1, matrix products, reproject(): jnp.einsum('nij,ncjl->ncil', rows_matrix, half_done, preferred_element_ty...  12.5 us
  transfers between devices with their start and end apart: 7, of which 3 were waited for; matrix products, arithmetic and copies ran while one was open for 28% of the time, Pallas kernels for 0%

profile of v1, /device:TPU:8, one launch (start us, length us, event | category | flops | bytes accessed | tf_op | source)
XLA Modules:
  0.0 459.3 jit_solution(5959264171993118642)
XLA Ops:
  2.6 4.3 all-to-all-start
  9.9 2.4 stack.32
  12.4 2.4 stack.33
  14.8 2.4 pad_maximum_fusion.1
  17.3 3.4 broadcast_in_dim.40
  20.7 8.2 %scatter_fusion.1 = bf16[128,2,4096]{2,1,0:T(2,128)(2,1)} fusion(bf16[128,2,4096]{2,1,0:T(2,128)(2,1)} %broadcast_in_dim.40, s32[64]{0:T(128)S(1)} %fusion.59, bf16[64,2,4096]{2,1,0:T(2,128)(2,1)S(1)} %pad_maximum_fusion.1), kind=kCustom, calls=%fused_computation.1 | custom fusion | bytes 3145984 | tf_op jit(solution)/shard_map/scatter | solution.py:126
  28.9 12.1 %all-to-all-start.2 = ((bf16[128,2,4096]{2,1,0:T(2,128)(2,1)}), bf16[128,2,4096]{2,1,0:T(2,128)(2,1)S(1)}, u32[]{:S(2)}, u32[]{:S(2)}) async-start(bf16[128,2,4096]{2,1,0:T(2,128)(2,1)} %scatter_fusion.1), calls=%async_computation.2 | async-start | bytes 4194304 | tf_op jit(solution)/shard_map/all_to_all | solution.py:129
  42.5 73.9 %while.10 = (s32[]{:T(128)}, bf16[16,1024]{1,0:T(8,128)(2,1)S(1)}, bf16[16,16,1024]{2,1,0:T(8,128)(2,1)S(1)}, bf16[16,256]{1,0:T(8,128)(2,1)S(1)}, bf16[2,256,25...) while((s32[]{:T(128)}, bf16[16,1024]{1,0:T(8,128)(2,1)S(1)}, ...), condition=%wide.region_3.4_spmd, body=%wide.region_2.3_spmd.sunk | while | flops 281285632 | bytes 1384577 | solution.py:46
  44.1 1.6 fusion.80
  48.7 1.6 fusion.80
  53.3 1.6 fusion.80
  57.9 1.6 fusion.80
  62.6 1.6 fusion.80
  67.2 1.6 fusion.80
  71.8 1.6 fusion.80
  76.4 1.6 fusion.80
  85.7 1.6 fusion.80
  90.3 1.6 fusion.80
  94.9 1.6 fusion.80
  99.5 1.6 fusion.80
  104.1 1.6 fusion.80
  113.4 1.6 fusion.80
  116.4 12.8 %all_gather.3 = bf16[16,4096]{1,0:T(8,128)(2,1)S(1)} all-gather(bf16[16,1024]{1,0:T(8,128)(2,1)S(1)} %get-tuple-element.47), channel_id=1, replica_groups=mesh['band'=4,'tile'=64] {'band'}, dimensions={1}, use_global_device_ids=true | all-gather | bytes 163840 | tf_op jit(solution)/shard_map/all_gather | solution.py:107
  130.1 2.4 broadcast_in_dim.20.clone
  132.5 4.3 broadcast_in_dim.16
  136.8 11.9 %scatter_fusion = bf16[128,5,4096]{2,1,0:T(8,128)(2,1)} fusion(bf16[128,5,4096]{2,1,0:T(8,128)(2,1)} %broadcast_in_dim.16, s32[64]{0:T(128)S(1)} %fusion.59, bf16[64,5,4096]{2,1,0:T(8,128)(2,1)} %bitcast.86), kind=kCustom, calls=%fused_computation | custom fusion | bytes 7864576 | tf_op jit(solution)/shard_map/scatter | solution.py:124
  148.7 10.5 %all-to-all-start.1 = ((bf16[128,5,4096]{2,1,0:T(8,128)(2,1)}), bf16[128,5,4096]{2,1,0:T(8,128)(2,1)}, u32[]{:S(2)}, u32[]{:S(2)}) async-start(bf16[128,5,4096]{2,1,0:T(8,128)(2,1)} %scatter_fusion), calls=%async_computation.1 | async-start | bytes 16777216 | tf_op jit(solution)/shard_map/all_to_all | solution.py:128
  159.2 4.0 copy.33
  163.3 2.7 fusion.60
  166.0 3.9 copy.43
  169.9 3.8 copy.44
  173.7 169.8 %all-to-all-done.1 = bf16[128,5,4096]{2,1,0:T(8,128)(2,1)} async-done(((bf16[128,5,4096]{2,1,0:T(8,128)(2,1)}), bf16[128,5,4096]{2,1,0:T(8,128)(2,1)}, u32[]{:S(2)}, u32[]{:S(2)}) %all-to-all-start.1) | async-done | bytes 5242912 | tf_op jit(solution)/shard_map/all_to_all | solution.py:128
  343.6 10.6 %copy.30 = bf16[128,5,4096]{0,2,1:T(8,128)(2,1)} copy(bf16[128,5,4096]{2,1,0:T(8,128)(2,1)} %all-to-all-done.1) | data formatting | bytes 10485760 | tf_op jit(solution)/shard_map/all_to_all | solution.py:128
  354.2 15.7 %copy.35 = bf16[128,5,64,64]{3,2,1,0:T(8,128)(2,1)} copy(bf16[128,5,64,64]{0,3,2,1:T(8,128)(2,1)} %bitcast.85) | data formatting | bytes 10485760 | tf_op jit(solution)/shard_map/reshape | solution.py:133
  369.9 12.5 %convert_bitcast_fusion = bf16[128,5,64,64]{2,3,1,0:T(8,128)(2,1)} fusion(bf16[128,5,64,64]{3,2,1,0:T(8,128)(2,1)} %copy.35, bf16[128,1,64,64]{3,2,0,1:T(8,128)(2,1)} %copy.44, bf16[128,1,64,64]{3,2,0,1:T(8,128)(2,1)S(1)} %copy.43), kind=kOutput, calls=%fused_computation.29 | convolution fusion | flops 676331520 | bytes 12582912 | tf_op jit(solution)/shard_map/nij,ncjl->ncil/dot_general | solution.py:53
  382.4 18.1 %copy.38 = bf16[128,5,64,64]{0,3,2,1:T(8,128)(2,1)} copy(bf16[128,5,64,64]{2,3,1,0:T(8,128)(2,1)} %convert_bitcast_fusion) | data formatting | bytes 10485760 | tf_op jit(solution)/shard_map/convert_element_type | solution.py:55
  402.0 1.9 fusion.48
  404.0 2.3 fusion.23
  406.3 7.8 %fusion.47 = (f32[4,4096]{1,0:T(4,128)S(1)}, f32[4,4096]{1,0:T(4,128)S(1)}) fusion(f32[4,4096]{1,0:T(4,128)S(1)} %broadcast_divide_fusion, f32[128,4096]{0,1:T(8,128)S(1)} %get-tuple-element.72, bf16[128,5,4096]{0,2,1:T(8,128)(2,1)S(1)} %bitcast.81), kind=kLoop, calls=%fused_computation.53 | loop fusion | flops 16744448 | bytes 6488064 | tf_op jit(solution)/shard_map/reduce_sum | solution.py:65
  414.1 7.6 %fusion.46 = (f32[4,4096]{1,0:T(4,128)S(1)}, f32[4,4096]{1,0:T(4,128)S(1)}) fusion(f32[4,4096]{1,0:T(4,128)S(1)} %add_divide_fusion.5, f32[128,4096]{0,1:T(8,128)S(1)} %get-tuple-element.72, bf16[128,5,4096]{0,2,1:T(8,128)(2,1)S(1)} %bitcast.82), kind=kLoop, calls=%fused_computation.52 | loop fusion | flops 16744448 | bytes 6488064 | tf_op jit(solution)/shard_map/reduce_sum | solution.py:65
  421.8 7.6 %fusion.45 = (f32[4,4096]{1,0:T(4,128)S(1)}, f32[4,4096]{1,0:T(4,128)S(1)}) fusion(f32[4,4096]{1,0:T(4,128)S(1)} %add_divide_fusion.4, f32[128,4096]{0,1:T(8,128)S(1)} %get-tuple-element.72, bf16[128,5,4096]{0,2,1:T(8,128)(2,1)S(1)} %bitcast.83), kind=kLoop, calls=%fused_computation.51 | loop fusion | flops 16744448 | bytes 6488064 | tf_op jit(solution)/shard_map/reduce_sum | solution.py:65
  429.4 7.6 %fusion.44 = (f32[4,4096]{1,0:T(4,128)S(1)}, f32[4,4096]{1,0:T(4,128)S(1)}) fusion(f32[4,4096]{1,0:T(4,128)S(1)} %add_divide_fusion.3, f32[128,4096]{0,1:T(8,128)S(1)} %get-tuple-element.72, bf16[128,5,4096]{0,2,1:T(8,128)(2,1)S(1)} %bitcast.84), kind=kLoop, calls=%fused_computation.50 | loop fusion | flops 16744448 | bytes 6488064 | tf_op jit(solution)/shard_map/reduce_sum | solution.py:65
  437.3 1.9 collective-permute-start
  439.2 3.3 collective-permute-start.1
  442.6 5.1 %collective-permute-done.1 = f32[4,64,1]{2,1,0:T(8,128)S(1)} collective-permute-done((f32[4,64,1]{2,1,0:T(8,128)S(1)}, f32[4,64,1]{2,1,0:T(8,128)S(1)}, u32[]{:S(2)}, u32[]{:S(2)}) %collective-permute-start.1) | collective-permute-done | bytes 1056 | tf_op jit(solution)/shard_map/ppermute | solution.py:19
  448.0 1.9 collective-permute-start.2
  449.9 2.4 collective-permute-start.3
  452.4 5.9 %collective-permute-done.3 = f32[4,64,1]{2,1,0:T(8,128)S(1)} collective-permute-done((f32[4,64,1]{2,1,0:T(8,128)S(1)}, f32[4,64,1]{2,1,0:T(8,128)S(1)}, u32[]{:S(2)}, u32[]{:S(2)}) %collective-permute-start.3) | collective-permute-done | bytes 1056 | tf_op jit(solution)/shard_map/ppermute | solution.py:19
  (168 shorter events, 62.1 us)
Async XLA Ops:
  0.0 28.9 %copy-start.4 = (s32[16]{0:T(128)S(1)}, s32[16]{0:T(128)}, u32[]{:S(2)}) copy-start(s32[16]{0:T(128)} %param.13) | copy-start | bytes 196
  2.6 26.3 %all-to-all-start = ((bf16[4,16,4,1024]{3,2,1,0:T(4,128)(2,1)}), bf16[4,16,4,1024]{3,2,1,0:T(4,128)(2,1)}, u32[]{:S(2)}, u32[]{:S(2)}) async-start(bf16[4,16,4,1024]{3,2,1,0:T(4,128)(2,1)} %pad_maximum_fusion.2), calls=%async_computation | async-start | bytes 1048576 | tf_op jit(solution)/shard_map/all_to_all | solution.py:100
  12.3 30.2 %copy-start.2 = (bf16[2,256,256]{2,1,0:T(8,128)(2,1)S(1)}, bf16[2,256,256]{2,1,0:T(8,128)(2,1)}, u32[]{:S(2)}) copy-start(bf16[2,256,256]{2,1,0:T(8,128)(2,1)} %param.18) | copy-start | bytes 786436
  12.3 30.2 %copy-start.3 = (bf16[16,256]{1,0:T(8,128)(2,1)S(1)}, bf16[16,256]{1,0:T(8,128)(2,1)}, u32[]{:S(2)}) copy-start(bf16[16,256]{1,0:T(8,128)(2,1)} %param.17) | copy-start | bytes 24580
  12.4 30.2 %copy-start.5 = (bf16[256]{0:T(256)(128)(2,1)S(1)}, bf16[256]{0:T(256)(128)(2,1)}, u32[]{:S(2)}) copy-start(bf16[256]{0:T(256)(128)(2,1)} %param.19) | copy-start | bytes 1540
  28.9 119.8 %all-to-all-start.2 = ((bf16[128,2,4096]{2,1,0:T(2,128)(2,1)}), bf16[128,2,4096]{2,1,0:T(2,128)(2,1)S(1)}, u32[]{:S(2)}, u32[]{:S(2)}) async-start(bf16[128,2,4096]{2,1,0:T(2,128)(2,1)} %scatter_fusion.1), calls=%async_computation.2 | async-start | bytes 4194304 | tf_op jit(solution)/shard_map/all_to_all | solution.py:129
  42.5 87.0 %copy-start.1 = (bf16[16,4,4096]{2,1,0:T(4,128)(2,1)S(1)}, bf16[16,4,4096]{2,1,0:T(4,128)(2,1)}, u32[]{:S(2)}) copy-start(bf16[16,4,4096]{2,1,0:T(4,128)(2,1)} %param.11) | copy-start | bytes 1572868
  148.7 194.8 %all-to-all-start.1 = ((bf16[128,5,4096]{2,1,0:T(8,128)(2,1)}), bf16[128,5,4096]{2,1,0:T(8,128)(2,1)}, u32[]{:S(2)}, u32[]{:S(2)}) async-start(bf16[128,5,4096]{2,1,0:T(8,128)(2,1)} %scatter_fusion), calls=%async_computation.1 | async-start | bytes 16777216 | tf_op jit(solution)/shard_map/all_to_all | solution.py:128
  400.5 3.4 copy-start
  437.3 5.3 %collective-permute-start = (f32[4,64,1]{2,1,0:T(8,128)S(1)}, f32[4,64,1]{2,1,0:T(8,128)S(1)}, u32[]{:S(2)}, u32[]{:S(2)}) collective-permute-start(f32[4,64,1]{2,1,0:T(8,128)S(1)} %get-tuple-element.82), channel_id=1, source_target_pairs={{1,0},{2,1},{3,2},{4,3},{5,4},{6,5},{7,6},{8,7},{9,8},{10,9},{11,1... | collective-permute-start | bytes 3080 | tf_op jit(solution)/shard_map/ppermute | solution.py:22
  439.2 8.4 %collective-permute-start.1 = (f32[4,64,1]{2,1,0:T(8,128)S(1)}, f32[4,64,1]{2,1,0:T(8,128)S(1)}, u32[]{:S(2)}, u32[]{:S(2)}) collective-permute-start(f32[4,64,1]{2,1,0:T(8,128)S(1)} %get-tuple-element.83), channel_id=1, source_target_pairs={{0,1},{1,2},{2,3},{3,4},{4,5},{5,6},{6,7},{7,8},{8,9},{9,10},{10,1... | collective-permute-start | bytes 3080 | tf_op jit(solution)/shard_map/ppermute | solution.py:19
  448.0 4.4 collective-permute-start.2
  449.9 8.4 %collective-permute-start.3 = (f32[4,64,1]{2,1,0:T(8,128)S(1)}, f32[4,64,1]{2,1,0:T(8,128)S(1)}, u32[]{:S(2)}, u32[]{:S(2)}) collective-permute-start(f32[4,64,1]{2,1,0:T(8,128)S(1)} %get-tuple-element.81), channel_id=1, source_target_pairs={{0,1},{1,2},{2,3},{3,4},{4,5},{5,6},{6,7},{7,8},{8,9},{9,10},{10,1... | collective-permute-start | bytes 3080 | tf_op jit(solution)/shard_map/ppermute | solution.py:19
